TPU v7x, 32 devices: a whole 2x2x4 slice. The times are simulated.
32 devices in a mesh: frame: 8 (over z, core), tok: 4 (over y, x).
Axes of the slice: x: 2, y: 2, z: 4, core: 2. Of those that a mesh axis runs over, the one named last changes fastest.
Arguments:
- stream: bfloat16 [8, 1024, 1152], P('frame', 'tok'), may hold values from -20 to 20
- queries: bfloat16 [8, 1024, 1152], P('frame', 'tok'), may hold values from -200 to 200
- key_vectors: bfloat16 [8, 1024, 1152], P('frame', 'tok'), may hold values from -6 to 6
- value_vectors: bfloat16 [8, 1024, 1152], P('frame', 'tok'), may hold values from -6 to 6
- modulation: float32 [8, 4, 1152], P('frame'), may hold values from -4 to 4
- output_weight: bfloat16 [1152, 1152], replicated, may hold values from -0.1875 to 0.1875
- output_bias: float32 [1152], replicated, may hold values from -3 to 3
- router_weight: bfloat16 [1152, 8], replicated, may hold values from -0.1875 to 0.1875
- expand_weight: bfloat16 [8, 1152, 4608], P('frame', None, 'tok'), may hold values from -0.1875 to 0.1875
- expand_bias: float32 [8, 4608], P('frame', 'tok'), may hold values from -3 to 3
- reduce_weight: bfloat16 [8, 4608, 1152], P('frame', 'tok'), may hold values from -0.09375 to 0.09375
- reduce_bias: float32 [8, 1152], P('frame'), may hold values from -3 to 3
- counts: int32 [8, 8], P(None, 'frame'), may hold values from 1 to 96, 256 in all within a row
- picked_rows: int32 [8, 8, 96], P(None, 'frame'), may hold values from 0 to 1023, as said below
Outputs:
- layer_out: bfloat16 [8, 1024, 1152], P('frame', 'tok')
Inputs may be any that keep to these rules, and one draw needn't show every extreme that they name: counts[e, g] slots of block (e, g) are used; the counts of one expert sum to 256. The entries of one block picked_rows[e, g, :] are distinct positions among the 1024 tokens of frame g; slots at or beyond counts[e, g] are unused.
All inputs are finite; a program needn't handle non-finite values.
Results may differ from a plain program's by a relative error of at most 0.0055.
Values may be sent and summed in bfloat16 or wider, within the bound.
A program may use at most 64 MiB of HBM per device.

v0:
```python
import math
import jax
import jax.numpy as jnp
from jax import lax
from jax.sharding import PartitionSpec as P

H = 16
HD = 72


def layer_norm(values):
    mean_val = jnp.mean(values, axis=-1, keepdims=True)
    centred = values - mean_val
    variance = jnp.mean(centred * centred, axis=-1, keepdims=True)
    return centred * lax.rsqrt(variance + 1e-06)


def head_attention(operands):
    head_queries, head_keys, head_values = operands
    length = head_queries.shape[1]
    block_rows = min(512, length)
    score_scale = 1.0 / math.sqrt(HD)

    def one_block(first_row):
        query_block = lax.dynamic_slice_in_dim(head_queries, first_row, block_rows, 1)
        scores = (
            lax.dot_general(
                query_block, head_keys, (((0,), (0,)), ((), ())), preferred_element_type=jnp.float32
            )
            * score_scale
        )
        scores = scores - jnp.max(scores, axis=1, keepdims=True)
        exponent = jnp.exp(scores)
        weights = (exponent / jnp.sum(exponent, axis=1, keepdims=True)).astype(jnp.bfloat16)
        return lax.dot_general(
            head_values, weights, (((1,), (1,)), ((), ())), preferred_element_type=jnp.float32
        ).astype(jnp.bfloat16)

    starts = jnp.arange(length // block_rows, dtype=jnp.int32) * block_rows
    blocks = lax.map(one_block, starts)
    return blocks.transpose(1, 0, 2).reshape(head_queries.shape[0], length)


def attend_items(pieces):
    outputs = lax.map(head_attention, (pieces[0][0], pieces[1][0], pieces[2][0]))
    return outputs[None]


def per_device(
    stream,
    queries,
    key_vectors,
    value_vectors,
    modulation,
    output_weight,
    output_bias,
    router_weight,
    expand_weight,
    expand_bias,
    reduce_weight,
    reduce_bias,
    counts,
    picked_rows,
):
    tok_groups = lax.axis_size("tok")
    tok_local = stream.shape[1]
    model_width = stream.shape[2]
    heads_local = H // tok_groups

    def to_heads(tensor):
        return tensor[0].reshape(tok_local, tok_groups, heads_local, HD).transpose(1, 2, 3, 0)

    attended = attend_items(
        (
            lax.all_to_all(to_heads(queries), "tok", split_axis=0, concat_axis=3, tiled=True),
            lax.all_to_all(to_heads(key_vectors), "tok", split_axis=0, concat_axis=3, tiled=True),
            lax.all_to_all(to_heads(value_vectors), "tok", split_axis=0, concat_axis=3, tiled=True),
        )
    )
    returned = lax.all_to_all(attended, "tok", split_axis=3, concat_axis=0, tiled=True)
    attended_rows = returned.transpose(3, 0, 1, 2).reshape(tok_local, model_width)
    projected = (
        jnp.dot(attended_rows, output_weight, preferred_element_type=jnp.float32) + output_bias
    )
    shares = modulation[0]
    residual = (stream[0].astype(jnp.float32) + shares[0] * projected).astype(jnp.bfloat16)
    normed = (layer_norm(residual.astype(jnp.float32)) * (1.0 + shares[2]) + shares[1]).astype(
        jnp.bfloat16
    )
    gate_values = jax.nn.sigmoid(jnp.dot(normed, router_weight, preferred_element_type=jnp.float32))
    slot_count = picked_rows.shape[2]
    local_pos = picked_rows[:, 0, :] - lax.axis_index("tok") * tok_local
    in_use = jnp.arange(slot_count, dtype=jnp.int32)[None, :] < counts
    on_shard = in_use & (local_pos >= 0) & (local_pos < tok_local)
    safe_pos = jnp.clip(local_pos, 0, tok_local - 1)
    chosen = jnp.take(normed, safe_pos, axis=0)
    chosen = jnp.where(on_shard[:, :, None], chosen, jnp.zeros_like(chosen))
    moved = lax.all_to_all(chosen, "frame", split_axis=0, concat_axis=1, tiled=True)
    expert_rows = lax.psum(moved.astype(jnp.float32).astype(jnp.bfloat16), "tok")
    hidden = jax.nn.gelu(
        jnp.einsum("erd,edf->erf", expert_rows, expand_weight, preferred_element_type=jnp.float32)
        + expand_bias[:, None, :],
        approximate=True,
    ).astype(jnp.bfloat16)
    partial_out = jnp.einsum(
        "erf,efd->erd", hidden, reduce_weight, preferred_element_type=jnp.float32
    )
    column_count = model_width // tok_groups
    summed = lax.psum_scatter(
        partial_out.astype(jnp.bfloat16), "tok", scatter_dimension=2, tiled=True
    ).astype(jnp.float32)
    bias_part = lax.dynamic_slice_in_dim(
        reduce_bias, lax.axis_index("tok") * column_count, column_count, 1
    )
    expert_out = (summed + bias_part[:, None, :]).astype(jnp.bfloat16)
    returned_cols = lax.all_to_all(expert_out, "frame", split_axis=1, concat_axis=0, tiled=True)
    returned_rows = lax.all_gather(returned_cols, "tok", axis=2, tiled=True)
    mix_weight = jnp.take_along_axis(gate_values.T, safe_pos, axis=1)
    mix_weight = jnp.where(on_shard, mix_weight, jnp.zeros_like(mix_weight)).astype(jnp.bfloat16)
    targets = jnp.arange(tok_local, dtype=jnp.int32)
    matches = (safe_pos.reshape(-1)[None, :] == targets[:, None]) & on_shard.reshape(-1)[None, :]
    scatter_table = jnp.where(matches, mix_weight.reshape(-1)[None, :], jnp.zeros((), jnp.bfloat16))
    expert_mix = jnp.dot(
        scatter_table, returned_rows.reshape(-1, model_width), preferred_element_type=jnp.float32
    )
    layer_out = (residual.astype(jnp.float32) + shares[3] * expert_mix).astype(jnp.bfloat16)
    return layer_out[None]


def solution(mesh):
    return jax.shard_map(
        per_device,
        mesh=mesh,
        in_specs=(
            P("frame", "tok", None),
            P("frame", "tok", None),
            P("frame", "tok", None),
            P("frame", "tok", None),
            P("frame", None, None),
            P(),
            P(),
            P(),
            P("frame", None, "tok"),
            P("frame", "tok"),
            P("frame", "tok", None),
            P("frame", None),
            P(None, "frame"),
            P(None, "frame", None),
        ),
        out_specs=P("frame", "tok", None),
        check_vma=False,
    )
```

profile of v0, /device:TPU:0, one launch (start us, length us, event | category | flops | bytes accessed | tf_op | source)
XLA Modules:
  0.0 382.8 jit_solution(11425842389973880382)
XLA Ops:
  6.5 2.3 copy.78
  8.8 5.2 %all-to-all-start = ((bf16[4,4,72,256]{3,2,1,0:T(8,128)(2,1)}), bf16[4,4,72,256]{3,2,1,0:T(8,128)(2,1)S(1)}, u32[]{:S(2)}, u32[]{:S(2)}) async-start(bf16[4,4,72,256]{3,2,1,0:T(8,128)(2,1)} %bitcast.128), calls=%async_computation | async-start | bytes 1179648 | tf_op jit(solution)/shard_map/all_to_all | solution.py:75
  14.0 2.1 copy.80
  16.1 6.6 %all-to-all-done = bf16[4,4,72,256]{3,2,1,0:T(8,128)(2,1)S(1)} async-done(((bf16[4,4,72,256]{3,2,1,0:T(8,128)(2,1)}), bf16[4,4,72,256]{3,2,1,0:T(8,128)(2,1)S(1)}, u32[]{:S(2)}, u32[]{:S(2)}) %all-to-all-start) | async-done | bytes 589856 | tf_op jit(solution)/shard_map/all_to_all | solution.py:75
  22.7 4.3 %all-to-all-start.1 = ((bf16[4,4,72,256]{3,2,1,0:T(8,128)(2,1)}), bf16[4,4,72,256]{3,2,1,0:T(8,128)(2,1)}, u32[]{:S(2)}, u32[]{:S(2)}) async-start(bf16[4,4,72,256]{3,2,1,0:T(8,128)(2,1)} %bitcast.127), calls=%async_computation.1 | async-start | bytes 1179648 | tf_op jit(solution)/shard_map/all_to_all | solution.py:76
  27.0 2.2 copy.82
  29.2 5.9 %all-to-all-done.1 = bf16[4,4,72,256]{3,2,1,0:T(8,128)(2,1)} async-done(((bf16[4,4,72,256]{3,2,1,0:T(8,128)(2,1)}), bf16[4,4,72,256]{3,2,1,0:T(8,128)(2,1)}, u32[]{:S(2)}, u32[]{:S(2)}) %all-to-all-start.1) | async-done | bytes 589856 | tf_op jit(solution)/shard_map/all_to_all | solution.py:76
  35.1 4.2 %all-to-all-start.2 = ((bf16[4,4,72,256]{3,2,1,0:T(8,128)(2,1)}), bf16[4,4,72,256]{3,2,1,0:T(8,128)(2,1)}, u32[]{:S(2)}, u32[]{:S(2)}) async-start(bf16[4,4,72,256]{3,2,1,0:T(8,128)(2,1)} %bitcast.126), calls=%async_computation.2 | async-start | bytes 1179648 | tf_op jit(solution)/shard_map/all_to_all | solution.py:77
  39.5 1.3 copy.79
  40.8 2.4 squeeze.27
  43.1 1.5 copy.81
  44.6 1.2 squeeze.28
  45.9 1.0 all-to-all-done.2
  46.9 1.5 copy.83
  48.4 1.3 squeeze.29
  49.6 45.9 %while.21 = (s32[]{:T(128)}, bf16[4,72,1024]{2,1,0:T(8,128)(2,1)}, bf16[4,72,1024]{2,1,0:T(8,128)(2,1)}, bf16[4,72,1024]{2,1,0:T(8,128)(2,1)}, bf16[4,72,1024]{2...) while((s32[]{:T(128)}, bf16[4,72,1024]{2,1,0:T(8,128)(2,1)}, ...), condition=%wide.region_5.6_spmd, body=%wide.region_0.5_spmd.sunk | while | flops 155749376 | bytes 8513900 | solution.py:45
  49.6 0.9 dynamic-slice_bitcast_fusion.5
  50.6 1.0 dynamic-slice_bitcast_fusion.6
  51.6 8.6 %while.22 = (s32[]{:T(128)}, bf16[2,72,512]{2,1,0:T(8,128)(2,1)S(1)}, s32[2]{0:T(128)S(1)}, bf16[72,1024]{1,0:T(8,128)(2,1)S(1)}, bf16[72,1024]{1,0:T(8,128)(2,1...) while((s32[]{:T(128)}, bf16[2,72,512]{2,1,0:T(8,128)(2,1)S(1)}, ...), condition=%wide.region_4.4_spmd, body=%wide.region_1.3_spmd.sunk | while | flops 155749376 | bytes 6744219 | solution.py:40
  55.2 0.7 fusion.60
  59.5 0.7 fusion.60
  61.1 0.9 dynamic-slice_bitcast_fusion.5
  62.1 1.0 dynamic-slice_bitcast_fusion.6
  63.1 8.6 %while.22 = (s32[]{:T(128)}, bf16[2,72,512]{2,1,0:T(8,128)(2,1)S(1)}, s32[2]{0:T(128)S(1)}, bf16[72,1024]{1,0:T(8,128)(2,1)S(1)}, bf16[72,1024]{1,0:T(8,128)(2,1...) while((s32[]{:T(128)}, bf16[2,72,512]{2,1,0:T(8,128)(2,1)S(1)}, ...), condition=%wide.region_4.4_spmd, body=%wide.region_1.3_spmd.sunk | while | flops 155749376 | bytes 6744219 | solution.py:40
  66.7 0.7 fusion.60
  71.0 0.7 fusion.60
  72.6 0.9 dynamic-slice_bitcast_fusion.5
  73.5 1.0 dynamic-slice_bitcast_fusion.6
  74.6 8.6 %while.22 = (s32[]{:T(128)}, bf16[2,72,512]{2,1,0:T(8,128)(2,1)S(1)}, s32[2]{0:T(128)S(1)}, bf16[72,1024]{1,0:T(8,128)(2,1)S(1)}, bf16[72,1024]{1,0:T(8,128)(2,1...) while((s32[]{:T(128)}, bf16[2,72,512]{2,1,0:T(8,128)(2,1)S(1)}, ...), condition=%wide.region_4.4_spmd, body=%wide.region_1.3_spmd.sunk | while | flops 155749376 | bytes 6744219 | solution.py:40
  78.2 0.7 fusion.60
  82.5 0.7 fusion.60
  84.1 0.9 dynamic-slice_bitcast_fusion.5
  85.0 1.0 dynamic-slice_bitcast_fusion.6
  86.0 8.6 %while.22 = (s32[]{:T(128)}, bf16[2,72,512]{2,1,0:T(8,128)(2,1)S(1)}, s32[2]{0:T(128)S(1)}, bf16[72,1024]{1,0:T(8,128)(2,1)S(1)}, bf16[72,1024]{1,0:T(8,128)(2,1...) while((s32[]{:T(128)}, bf16[2,72,512]{2,1,0:T(8,128)(2,1)S(1)}, ...), condition=%wide.region_4.4_spmd, body=%wide.region_1.3_spmd.sunk | while | flops 155749376 | bytes 6744219 | solution.py:40
  89.7 0.7 fusion.60
  94.0 0.7 fusion.60
  95.6 2.3 copy.84
  97.9 4.4 %all-to-all-start.3 = ((bf16[1,4,72,1024]{2,1,0,3:T(4,128)(2,1)}), bf16[1,4,72,1024]{2,1,0,3:T(4,128)(2,1)}, u32[]{:S(2)}, u32[]{:S(2)}) async-start(bf16[1,4,72,1024]{2,1,0,3:T(4,128)(2,1)} %bitcast.123), calls=%async_computation.3 | async-start | bytes 2097152 | tf_op jit(solution)/shard_map/all_to_all | solution.py:80
  102.5 11.4 %all-to-all-done.3 = bf16[1,4,72,1024]{2,1,0,3:T(4,128)(2,1)} async-done(((bf16[1,4,72,1024]{2,1,0,3:T(4,128)(2,1)}), bf16[1,4,72,1024]{2,1,0,3:T(4,128)(2,1)}, u32[]{:S(2)}, u32[]{:S(2)}) %all-to-all-start.3) | async-done | bytes 589856 | tf_op jit(solution)/shard_map/all_to_all | solution.py:80
  113.9 1.5 copy.86
  115.4 3.0 fusion.44
  118.7 0.7 copy-done.1
  119.7 3.7 gather_fusion
  123.4 1.9 select_select_fusion
  125.3 46.8 %all_to_all.87 = bf16[8,96,1152]{2,1,0:T(8,128)(2,1)} all-to-all(bf16[8,96,1152]{2,1,0:T(8,128)(2,1)S(1)} %select_select_fusion), channel_id=1, replica_groups=mesh['frame'=8,'tok'=4] {'frame'}, dimensions={0} | all-to-all | bytes 3538944 | tf_op jit(solution)/shard_map/all_to_all | solution.py:98
  172.8 61.5 %all-reduce.2.cloned.1.call-done = bf16[768,1152]{1,0:T(8,128)(2,1)} async-done(((bf16[768,1152]{1,0:T(8,128)(2,1)}), bf16[768,1152]{1,0:T(8,128)(2,1)}) %all-reduce.2.cloned.1.call-update) | async-done | bytes 1769488 | tf_op jit(solution)/shard_map/psum | solution.py:99
  234.2 8.8 %fusion.15 = bf16[1,768,1152]{2,1,0:T(8,128)(2,1)} fusion(bf16[1,1152,1152]{2,1,0:T(8,128)(2,1)S(1)} %copy-done, bf16[768,1152]{1,0:T(8,128)(2,1)} %all-reduce.2.cloned.1.call-done, bf16[1,1152,1152]{2,1,0:T(8,128)(2,1)} %param.26, f32[1152]{0:T(1024)S(1)} %reduce.5), kind=kOutput, calls=%fused_computation.29 | convolution fusion | flops 4086595584 | bytes 8851968 | tf_op jit(solution)/shard_map/erf,efd->erd/dot_general | solution.py:105
  243.0 8.8 %copy.95 = bf16[1,768,1152]{1,0,2:T(2,128)(2,1)} copy(bf16[1,768,1152]{2,1,0:T(8,128)(2,1)} %fusion.15) | data formatting | bytes 3538944
  251.9 3.5 copy.103
  255.5 0.8 dynamic-slice_reduce_fusion
  256.2 31.8 %reduce-scatter.4.cloned.1.call-done = bf16[288,768]{1,0:T(8,128)(2,1)} async-done(((bf16[1152,768]{1,0:T(8,128)(2,1)}), bf16[288,768]{1,0:T(8,128)(2,1)}) %reduce-scatter.4.cloned.1.call-update) | async-done | bytes 442384
  288.0 1.5 reshape_bitcast_fusion
  289.5 0.9 add_convert_fusion.1
  290.4 4.6 %copy.90 = bf16[1,768,288]{2,0,1:T(2,128)(2,1)} copy(bf16[1,768,288]{1,2,0:T(8,128)(2,1)} %add_convert_fusion.1) | data formatting | bytes 884736 | tf_op jit(solution)/shard_map/convert_element_type | solution.py:115
  295.5 6.1 %reduce.13 = bf16[768,288]{1,0:T(8,128)(2,1)} reduce(bf16[768,1,288]{2,1,0:T(2,128)(2,1)} %bitcast.121, bf16[]{:T(256)} %broadcast.265), dimensions={1}, to_apply=%bitcast.92.reduce_sub_computation | reduce | bytes 884738
  301.6 2.6 reshape.249
  304.3 18.3 %all_to_all.88 = bf16[8,2,13824]{2,1,0:T(2,128)(2,1)} all-to-all(bf16[8,2,13824]{2,1,0:T(2,128)(2,1)} %reshape.249), channel_id=1, replica_groups=mesh['frame'=8,'tok'=4] {'frame'}, dimensions={0} | all-to-all | bytes 884736 | tf_op jit(solution)/shard_map/all_to_all | solution.py:116
  322.5 3.8 reshape.250
  326.3 4.5 %copy.91 = bf16[1,768,288]{1,2,0:T(8,128)(2,1)} copy(bf16[1,768,288]{2,0,1:T(2,128)(2,1)} %bitcast.122) | data formatting | bytes 884736 | tf_op jit(solution)/shard_map/all_to_all | solution.py:116
  330.8 2.5 all_to_all.80
  334.0 6.5 %gather_fusion.1 = bf16[768]{0:T(1024)(128)(2,1)S(1)} fusion(bf16[8,256]{1,0:T(8,128)(2,1)S(1)} %fusion.28, s32[768]{0:T(1024)S(1)} %reshape.231), kind=kCustom, calls=%fused_computation.1 | custom fusion | bytes 9216 | tf_op jit(solution)/shard_map/jit(take_along_axis)/gather | solution.py:118
  340.5 28.3 %all-gather.2.cloned.1.call-done = bf16[8,96,1152]{1,0,2:T(8,128)(2,1)} async-done(((bf16[8,96,288]{1,0,2:T(8,128)(2,1)}), bf16[8,96,1152]{1,0,2:T(8,128)(2,1)}) %all-gather.2.cloned.1.call-update) | async-done | bytes 1769488 | tf_op jit(solution)/shard_map/all_gather | solution.py:117
  368.8 4.2 %copy.92 = bf16[8,96,1152]{2,1,0:T(8,128)(2,1)} copy(bf16[8,96,1152]{1,0,2:T(8,128)(2,1)} %all-gather.2.cloned.1.call-done) | data formatting | bytes 3538944 | tf_op jit(solution)/shard_map/all_gather | solution.py:117
  373.0 3.3 fusion.24
  (87 shorter events, 20.6 us)
Async XLA Ops:
  6.5 227.7 %copy-start = (bf16[1,1152,1152]{2,1,0:T(8,128)(2,1)S(1)}, bf16[1,1152,1152]{2,1,0:T(8,128)(2,1)}, u32[]{:S(2)}) copy-start(bf16[1,1152,1152]{2,1,0:T(8,128)(2,1)} %param.28) | copy-start | bytes 7962628
  8.8 13.9 %all-to-all-start = ((bf16[4,4,72,256]{3,2,1,0:T(8,128)(2,1)}), bf16[4,4,72,256]{3,2,1,0:T(8,128)(2,1)S(1)}, u32[]{:S(2)}, u32[]{:S(2)}) async-start(bf16[4,4,72,256]{3,2,1,0:T(8,128)(2,1)} %bitcast.128), calls=%async_computation | async-start | bytes 1179648 | tf_op jit(solution)/shard_map/all_to_all | solution.py:75
  14.0 15.2 %copy-start.5 = (s32[8,1,96]{2,1,0:T(1,128)S(1)}, s32[8,1,96]{2,1,0:T(1,128)}, u32[]{:S(2)}) copy-start(s32[8,1,96]{2,1,0:T(1,128)} %param.31) | copy-start | bytes 9220
  22.7 16.7 %copy-start.3 = (f32[1,4,1152]{2,1,0:T(4,128)S(1)}, f32[1,4,1152]{2,1,0:T(4,128)}, u32[]{:S(2)}) copy-start(f32[1,4,1152]{2,1,0:T(4,128)} %param.22) | copy-start | bytes 55300
  22.7 12.4 %all-to-all-start.1 = ((bf16[4,4,72,256]{3,2,1,0:T(8,128)(2,1)}), bf16[4,4,72,256]{3,2,1,0:T(8,128)(2,1)}, u32[]{:S(2)}, u32[]{:S(2)}) async-start(bf16[4,4,72,256]{3,2,1,0:T(8,128)(2,1)} %bitcast.127), calls=%async_computation.1 | async-start | bytes 1179648 | tf_op jit(solution)/shard_map/all_to_all | solution.py:76
  35.1 11.7 %all-to-all-start.2 = ((bf16[4,4,72,256]{3,2,1,0:T(8,128)(2,1)}), bf16[4,4,72,256]{3,2,1,0:T(8,128)(2,1)}, u32[]{:S(2)}, u32[]{:S(2)}) async-start(bf16[4,4,72,256]{3,2,1,0:T(8,128)(2,1)} %bitcast.126), calls=%async_computation.2 | async-start | bytes 1179648 | tf_op jit(solution)/shard_map/all_to_all | solution.py:77
  95.6 6.8 %copy-start.6 = (s32[8,1]{0,1:T(1,128)S(1)}, s32[8,1]{0,1:T(1,128)}, u32[]{:S(2)}) copy-start(s32[8,1]{0,1:T(1,128)} %param.30) | copy-start | bytes 100
  97.9 17.4 %copy-start.7 = (f32[1152]{0:T(1024)S(1)}, f32[1152]{0:T(1024)}, u32[]{:S(2)}) copy-start(f32[1152]{0:T(1024)} %param.24) | copy-start | bytes 13828
  97.9 15.9 %all-to-all-start.3 = ((bf16[1,4,72,1024]{2,1,0,3:T(4,128)(2,1)}), bf16[1,4,72,1024]{2,1,0,3:T(4,128)(2,1)}, u32[]{:S(2)}, u32[]{:S(2)}) async-start(bf16[1,4,72,1024]{2,1,0,3:T(4,128)(2,1)} %bitcast.123), calls=%async_computation.3 | async-start | bytes 2097152 | tf_op jit(solution)/shard_map/all_to_all | solution.py:80
  102.3 131.9 %all-reduce.2.cloned.1.call-start = ((), (), s32[]{:S(2)}) async-start(), calls=%async_computation.7 | async-start | bytes 3538944 | tf_op jit(solution)/shard_map/psum | solution.py:99
  118.4 1.0 copy-start.1
  172.0 0.7 copy-start.4
  172.1 116.0 %reduce-scatter.4.cloned.1.call-start = ((), (), s32[]{:S(2)}) async-start(), calls=%async_computation.9 | async-start | bytes 2211840
  255.4 113.4 %all-gather.2.cloned.1.call-start = ((), (), s32[]{:S(2)}) async-start(), calls=%async_computation.8 | async-start | bytes 2949120 | tf_op jit(solution)/shard_map/all_gather | solution.py:117
  326.3 7.4 %copy-start.2 = (bf16[1152,8]{0,1:T(8,128)(2,1)S(1)}, bf16[1152,8]{0,1:T(8,128)(2,1)}, u32[]{:S(2)}) copy-start(bf16[1152,8]{0,1:T(8,128)(2,1)} %param.25) | copy-start | bytes 55300
Sparse Core Ops, SparseCore 0:
  172.2 61.9 all-reduce.1
  255.5 32.4 reduce-scatter.3
  333.4 35.2 all-gather.1
where the time goes:
time: 385 us; the launch traced here: 383 us
  waiting for transfers between devices  147 us (38%)
  local copies, waits for them, and re-layouts  84.9 us (22%)
  blocking collectives  65.1 us (17%)
  matrix products  25.9 us (7%)
  starting transfers between devices  18.3 us (5%)
  loops' own time  14.9 us (4%)
  other arithmetic  13.9 us (4%)
  between operations  13.3 us (3%)
    psum x1, waiting for transfers between devices, per_device(): lax.psum(moved.astype(jnp.float32).astype(jnp.bfloat16), 'tok')  61.5 us
    all_to_all x1, blocking collectives, per_device(): lax.all_to_all(chosen, 'frame', split_axis=0, concat_axis=1, tiled=True)  46.8 us
    unnamed x4, waiting for transfers between devices  31.9 us
    unnamed x25, local copies, waits for them, and re-layouts  28.5 us
    all_gather x1, waiting for transfers between devices, per_device(): returned_rows = lax.all_gather(returned_cols, 'tok', axis=2, tiled=True)  28.3 us
    all_to_all x1, blocking collectives, per_device(): lax.all_to_all(expert_out, 'frame', split_axis=1, concat_axis=0, tiled=True)  18.3 us
    another operation x4, loops' own time, head_attention(): blocks = lax.map(one_block, starts)  14.8 us
    all_to_all x1, waiting for transfers between devices, per_device(): lax.all_to_all(attended, 'tok', split_axis=3, concat_axis=0, tiled=True)  11.4 us
  transfers between devices with their start and end apart: 7, of which 7 were waited for; matrix products, arithmetic and copies ran while one was open for 5% of the time, Pallas kernels for 0%

commit v1 on v0

--- a/solution.py
+++ b/solution.py
@@ -96,7 +96,9 @@
     chosen = jnp.take(normed, safe_pos, axis=0)
     chosen = jnp.where(on_shard[:, :, None], chosen, jnp.zeros_like(chosen))
     moved = lax.all_to_all(chosen, "frame", split_axis=0, concat_axis=1, tiled=True)
-    expert_rows = lax.psum(moved.astype(jnp.float32).astype(jnp.bfloat16), "tok")
+    block_in = moved.astype(jnp.float32).astype(jnp.bfloat16)
+    out_arr = jax.lax.all_gather(block_in, "tok")
+    expert_rows = jnp.sum(out_arr, axis=0)
     hidden = jax.nn.gelu(
         jnp.einsum("erd,edf->erf", expert_rows, expand_weight, preferred_element_type=jnp.float32)
         + expand_bias[:, None, :],

time: 385 us -> 403 us (1.047)
  waiting for transfers between devices: 147 us -> 159 us
  other arithmetic: 13.9 us -> 19.7 us
    all_gather x0 -> x1, waiting for transfers between devices: none -> 74 us  [per_device(): out_arr = jax.lax.all_gather(block_in, 'tok')]
    psum x1 -> x0, waiting for transfers between devices: 61.5 us -> none  [per_device(): lax.psum(moved.astype(jnp.float32).astype(jnp.bfloat16), 'tok')]
    reduce_sum x0 -> x1, other arithmetic: none -> 5.83 us  [per_device(): expert_rows = jnp.sum(out_arr, axis=0)]
where the time goes in v1:
time: 403 us; the launch traced here: 401 us
  waiting for transfers between devices  159 us (39%)
  local copies, waits for them, and re-layouts  84.9 us (21%)
  blocking collectives  65.1 us (16%)
  matrix products  25.9 us (6%)
  other arithmetic  19.7 us (5%)
  starting transfers between devices  18.3 us (5%)
  loops' own time  14.9 us (4%)
  between operations  13.3 us (3%)
    all_gather x1, waiting for transfers between devices, per_device(): out_arr = jax.lax.all_gather(block_in, 'tok')  74 us
    all_to_all x1, blocking collectives, per_device(): lax.all_to_all(chosen, 'frame', split_axis=0, concat_axis=1, tiled=True)  46.8 us
    unnamed x4, waiting for transfers between devices  31.9 us
    unnamed x25, local copies, waits for them, and re-layouts  28.6 us
    all_gather x1, waiting for transfers between devices, per_device(): returned_rows = lax.all_gather(returned_cols, 'tok', axis=2, tiled=True)  28.3 us
    all_to_all x1, blocking collectives, per_device(): lax.all_to_all(expert_out, 'frame', split_axis=1, concat_axis=0, tiled=True)  18.3 us
    another operation x4, loops' own time, head_attention(): blocks = lax.map(one_block, starts)  14.8 us
    all_to_all x1, waiting for transfers between devices, per_device(): lax.all_to_all(attended, 'tok', split_axis=3, concat_axis=0, tiled=True)  11.4 us
  transfers between devices with their start and end apart: 7, of which 7 were waited for; matrix products, arithmetic and copies ran while one was open for 5% of the time, Pallas kernels for 0%

profile of v1, /device:TPU:0, one launch (start us, length us, event | category | flops | bytes accessed | tf_op | source)
XLA Modules:
  0.0 401.3 jit_solution(9132208707262150785)
XLA Ops:
  6.5 2.3 copy.78
  8.8 5.2 %all-to-all-start = ((bf16[4,4,72,256]{3,2,1,0:T(8,128)(2,1)}), bf16[4,4,72,256]{3,2,1,0:T(8,128)(2,1)S(1)}, u32[]{:S(2)}, u32[]{:S(2)}) async-start(bf16[4,4,72,256]{3,2,1,0:T(8,128)(2,1)} %bitcast.128), calls=%async_computation | async-start | bytes 1179648 | tf_op jit(solution)/shard_map/all_to_all | solution.py:75
  14.0 2.1 copy.80
  16.1 6.6 %all-to-all-done = bf16[4,4,72,256]{3,2,1,0:T(8,128)(2,1)S(1)} async-done(((bf16[4,4,72,256]{3,2,1,0:T(8,128)(2,1)}), bf16[4,4,72,256]{3,2,1,0:T(8,128)(2,1)S(1)}, u32[]{:S(2)}, u32[]{:S(2)}) %all-to-all-start) | async-done | bytes 589856 | tf_op jit(solution)/shard_map/all_to_all | solution.py:75
  22.7 4.3 %all-to-all-start.1 = ((bf16[4,4,72,256]{3,2,1,0:T(8,128)(2,1)}), bf16[4,4,72,256]{3,2,1,0:T(8,128)(2,1)}, u32[]{:S(2)}, u32[]{:S(2)}) async-start(bf16[4,4,72,256]{3,2,1,0:T(8,128)(2,1)} %bitcast.127), calls=%async_computation.1 | async-start | bytes 1179648 | tf_op jit(solution)/shard_map/all_to_all | solution.py:76
  27.0 2.2 copy.82
  29.2 5.9 %all-to-all-done.1 = bf16[4,4,72,256]{3,2,1,0:T(8,128)(2,1)} async-done(((bf16[4,4,72,256]{3,2,1,0:T(8,128)(2,1)}), bf16[4,4,72,256]{3,2,1,0:T(8,128)(2,1)}, u32[]{:S(2)}, u32[]{:S(2)}) %all-to-all-start.1) | async-done | bytes 589856 | tf_op jit(solution)/shard_map/all_to_all | solution.py:76
  35.1 4.2 %all-to-all-start.2 = ((bf16[4,4,72,256]{3,2,1,0:T(8,128)(2,1)}), bf16[4,4,72,256]{3,2,1,0:T(8,128)(2,1)}, u32[]{:S(2)}, u32[]{:S(2)}) async-start(bf16[4,4,72,256]{3,2,1,0:T(8,128)(2,1)} %bitcast.126), calls=%async_computation.2 | async-start | bytes 1179648 | tf_op jit(solution)/shard_map/all_to_all | solution.py:77
  39.5 1.3 copy.79
  40.8 2.4 squeeze.27
  43.1 1.5 copy.81
  44.6 1.2 squeeze.28
  45.9 1.0 all-to-all-done.2
  46.9 1.5 copy.83
  48.4 1.3 squeeze.29
  49.6 45.9 %while.21 = (s32[]{:T(128)}, bf16[4,72,1024]{2,1,0:T(8,128)(2,1)}, bf16[4,72,1024]{2,1,0:T(8,128)(2,1)}, bf16[4,72,1024]{2,1,0:T(8,128)(2,1)}, bf16[4,72,1024]{2...) while((s32[]{:T(128)}, bf16[4,72,1024]{2,1,0:T(8,128)(2,1)}, ...), condition=%wide.region_5.6_spmd, body=%wide.region_0.5_spmd.sunk | while | flops 155749376 | bytes 8513900 | solution.py:45
  49.6 0.9 dynamic-slice_bitcast_fusion.5
  50.6 1.0 dynamic-slice_bitcast_fusion.6
  51.6 8.6 %while.22 = (s32[]{:T(128)}, bf16[2,72,512]{2,1,0:T(8,128)(2,1)S(1)}, s32[2]{0:T(128)S(1)}, bf16[72,1024]{1,0:T(8,128)(2,1)S(1)}, bf16[72,1024]{1,0:T(8,128)(2,1...) while((s32[]{:T(128)}, bf16[2,72,512]{2,1,0:T(8,128)(2,1)S(1)}, ...), condition=%wide.region_4.4_spmd, body=%wide.region_1.3_spmd.sunk | while | flops 155749376 | bytes 6744219 | solution.py:40
  55.2 0.7 fusion.60
  59.5 0.7 fusion.60
  61.1 0.9 dynamic-slice_bitcast_fusion.5
  62.1 1.0 dynamic-slice_bitcast_fusion.6
  63.1 8.6 %while.22 = (s32[]{:T(128)}, bf16[2,72,512]{2,1,0:T(8,128)(2,1)S(1)}, s32[2]{0:T(128)S(1)}, bf16[72,1024]{1,0:T(8,128)(2,1)S(1)}, bf16[72,1024]{1,0:T(8,128)(2,1...) while((s32[]{:T(128)}, bf16[2,72,512]{2,1,0:T(8,128)(2,1)S(1)}, ...), condition=%wide.region_4.4_spmd, body=%wide.region_1.3_spmd.sunk | while | flops 155749376 | bytes 6744219 | solution.py:40
  66.7 0.7 fusion.60
  71.0 0.7 fusion.60
  72.6 0.9 dynamic-slice_bitcast_fusion.5
  73.5 1.0 dynamic-slice_bitcast_fusion.6
  74.6 8.6 %while.22 = (s32[]{:T(128)}, bf16[2,72,512]{2,1,0:T(8,128)(2,1)S(1)}, s32[2]{0:T(128)S(1)}, bf16[72,1024]{1,0:T(8,128)(2,1)S(1)}, bf16[72,1024]{1,0:T(8,128)(2,1...) while((s32[]{:T(128)}, bf16[2,72,512]{2,1,0:T(8,128)(2,1)S(1)}, ...), condition=%wide.region_4.4_spmd, body=%wide.region_1.3_spmd.sunk | while | flops 155749376 | bytes 6744219 | solution.py:40
  78.2 0.7 fusion.60
  82.5 0.7 fusion.60
  84.1 0.9 dynamic-slice_bitcast_fusion.5
  85.0 1.0 dynamic-slice_bitcast_fusion.6
  86.0 8.6 %while.22 = (s32[]{:T(128)}, bf16[2,72,512]{2,1,0:T(8,128)(2,1)S(1)}, s32[2]{0:T(128)S(1)}, bf16[72,1024]{1,0:T(8,128)(2,1)S(1)}, bf16[72,1024]{1,0:T(8,128)(2,1...) while((s32[]{:T(128)}, bf16[2,72,512]{2,1,0:T(8,128)(2,1)S(1)}, ...), condition=%wide.region_4.4_spmd, body=%wide.region_1.3_spmd.sunk | while | flops 155749376 | bytes 6744219 | solution.py:40
  94.0 0.7 fusion.60
  95.6 2.3 copy.84
  97.9 4.4 %all-to-all-start.3 = ((bf16[1,4,72,1024]{2,1,0,3:T(4,128)(2,1)}), bf16[1,4,72,1024]{2,1,0,3:T(4,128)(2,1)}, u32[]{:S(2)}, u32[]{:S(2)}) async-start(bf16[1,4,72,1024]{2,1,0,3:T(4,128)(2,1)} %bitcast.123), calls=%async_computation.3 | async-start | bytes 2097152 | tf_op jit(solution)/shard_map/all_to_all | solution.py:80
  102.5 11.4 %all-to-all-done.3 = bf16[1,4,72,1024]{2,1,0,3:T(4,128)(2,1)} async-done(((bf16[1,4,72,1024]{2,1,0,3:T(4,128)(2,1)}), bf16[1,4,72,1024]{2,1,0,3:T(4,128)(2,1)}, u32[]{:S(2)}, u32[]{:S(2)}) %all-to-all-start.3) | async-done | bytes 589856 | tf_op jit(solution)/shard_map/all_to_all | solution.py:80
  113.9 1.5 copy.86
  115.4 3.0 fusion.44
  118.7 0.8 copy-done.1
  119.8 3.7 gather_fusion
  123.5 1.9 select_select_fusion
  125.3 46.8 %all_to_all.84 = bf16[8,96,1152]{2,1,0:T(8,128)(2,1)} all-to-all(bf16[8,96,1152]{2,1,0:T(8,128)(2,1)S(1)} %select_select_fusion), channel_id=1, replica_groups=mesh['frame'=8,'tok'=4] {'frame'}, dimensions={0} | all-to-all | bytes 3538944 | tf_op jit(solution)/shard_map/all_to_all | solution.py:98
  172.8 74.0 %all-gather.3.cloned.1.call-done = bf16[4,1,768,1152]{3,2,1,0:T(8,128)(2,1)} async-done(((bf16[1,1,768,1152]{3,2,1,0:T(8,128)(2,1)}), bf16[4,1,768,1152]{3,2,1,0:T(8,128)(2,1)}) %all-gather.3.cloned.1.call-update) | async-done | bytes 7077904 | tf_op jit(solution)/shard_map/all_gather | solution.py:100
  246.8 5.8 %reduce_sum.41 = bf16[768,1152]{1,0:T(8,128)(2,1)} reduce(bf16[4,1,768,1152]{3,2,1,0:T(8,128)(2,1)} %all-gather.3.cloned.1.call-done, bf16[]{:T(256)} %constant.42.clone.1), dimensions={0,1}, to_apply=%region_8.9 | reduce | flops 2654208 | bytes 8847362 | tf_op jit(solution)/shard_map/reduce_sum | solution.py:101
  252.7 8.8 %fusion.15 = bf16[1,768,1152]{2,1,0:T(8,128)(2,1)} fusion(bf16[1,1152,1152]{2,1,0:T(8,128)(2,1)S(1)} %copy-done, bf16[768,1152]{1,0:T(8,128)(2,1)} %reduce_sum.41, bf16[1,1152,1152]{2,1,0:T(8,128)(2,1)} %param.26, f32[1152]{0:T(1024)S(1)} %reduce.7), kind=kOutput, calls=%fused_computation.29 | convolution fusion | flops 4086595584 | bytes 8851968 | tf_op jit(solution)/shard_map/erf,efd->erd/dot_general | solution.py:107
  261.5 8.8 %copy.95 = bf16[1,768,1152]{1,0,2:T(2,128)(2,1)} copy(bf16[1,768,1152]{2,1,0:T(8,128)(2,1)} %fusion.15) | data formatting | bytes 3538944
  270.3 3.5 copy.103
  273.9 0.8 dynamic-slice_reduce_fusion
  274.7 31.8 %reduce-scatter.4.cloned.1.call-done = bf16[288,768]{1,0:T(8,128)(2,1)} async-done(((bf16[1152,768]{1,0:T(8,128)(2,1)}), bf16[288,768]{1,0:T(8,128)(2,1)}) %reduce-scatter.4.cloned.1.call-update) | async-done | bytes 442384
  306.5 1.5 reshape_bitcast_fusion
  307.9 0.9 add_convert_fusion.1
  308.8 4.6 %copy.90 = bf16[1,768,288]{2,0,1:T(2,128)(2,1)} copy(bf16[1,768,288]{1,2,0:T(8,128)(2,1)} %add_convert_fusion.1) | data formatting | bytes 884736 | tf_op jit(solution)/shard_map/convert_element_type | solution.py:117
  314.0 6.1 %reduce.15 = bf16[768,288]{1,0:T(8,128)(2,1)} reduce(bf16[768,1,288]{2,1,0:T(2,128)(2,1)} %bitcast.121, bf16[]{:T(256)} %broadcast.265), dimensions={1}, to_apply=%bitcast.92.reduce_sub_computation | reduce | bytes 884738
  320.1 2.6 reshape.248
  322.7 18.3 %all_to_all.85 = bf16[8,2,13824]{2,1,0:T(2,128)(2,1)} all-to-all(bf16[8,2,13824]{2,1,0:T(2,128)(2,1)} %reshape.248), channel_id=1, replica_groups=mesh['frame'=8,'tok'=4] {'frame'}, dimensions={0} | all-to-all | bytes 884736 | tf_op jit(solution)/shard_map/all_to_all | solution.py:118
  341.0 3.8 reshape.249
  344.7 4.5 %copy.91 = bf16[1,768,288]{1,2,0:T(8,128)(2,1)} copy(bf16[1,768,288]{2,0,1:T(2,128)(2,1)} %bitcast.122) | data formatting | bytes 884736 | tf_op jit(solution)/shard_map/all_to_all | solution.py:118
  349.3 2.5 all_to_all.77
  352.4 6.5 %gather_fusion.1 = bf16[768]{0:T(1024)(128)(2,1)S(1)} fusion(bf16[8,256]{1,0:T(8,128)(2,1)S(1)} %fusion.28, s32[768]{0:T(1024)S(1)} %reshape.230), kind=kCustom, calls=%fused_computation.1 | custom fusion | bytes 9216 | tf_op jit(solution)/shard_map/jit(take_along_axis)/gather | solution.py:120
  358.9 28.3 %all-gather.5.cloned.1.call-done = bf16[8,96,1152]{1,0,2:T(8,128)(2,1)} async-done(((bf16[8,96,288]{1,0,2:T(8,128)(2,1)}), bf16[8,96,1152]{1,0,2:T(8,128)(2,1)}) %all-gather.5.cloned.1.call-update) | async-done | bytes 1769488 | tf_op jit(solution)/shard_map/all_gather | solution.py:119
  387.2 4.2 %copy.92 = bf16[8,96,1152]{2,1,0:T(8,128)(2,1)} copy(bf16[8,96,1152]{1,0,2:T(8,128)(2,1)} %all-gather.5.cloned.1.call-done) | data formatting | bytes 3538944 | tf_op jit(solution)/shard_map/all_gather | solution.py:119
  391.4 3.3 fusion.24
  (88 shorter events, 21.3 us)
Async XLA Ops:
  6.5 246.1 %copy-start = (bf16[1,1152,1152]{2,1,0:T(8,128)(2,1)S(1)}, bf16[1,1152,1152]{2,1,0:T(8,128)(2,1)}, u32[]{:S(2)}) copy-start(bf16[1,1152,1152]{2,1,0:T(8,128)(2,1)} %param.28) | copy-start | bytes 7962628
  8.8 13.9 %all-to-all-start = ((bf16[4,4,72,256]{3,2,1,0:T(8,128)(2,1)}), bf16[4,4,72,256]{3,2,1,0:T(8,128)(2,1)S(1)}, u32[]{:S(2)}, u32[]{:S(2)}) async-start(bf16[4,4,72,256]{3,2,1,0:T(8,128)(2,1)} %bitcast.128), calls=%async_computation | async-start | bytes 1179648 | tf_op jit(solution)/shard_map/all_to_all | solution.py:75
  14.0 15.2 %copy-start.5 = (s32[8,1,96]{2,1,0:T(1,128)S(1)}, s32[8,1,96]{2,1,0:T(1,128)}, u32[]{:S(2)}) copy-start(s32[8,1,96]{2,1,0:T(1,128)} %param.31) | copy-start | bytes 9220
  22.7 16.7 %copy-start.3 = (f32[1,4,1152]{2,1,0:T(4,128)S(1)}, f32[1,4,1152]{2,1,0:T(4,128)}, u32[]{:S(2)}) copy-start(f32[1,4,1152]{2,1,0:T(4,128)} %param.22) | copy-start | bytes 55300
  22.7 12.4 %all-to-all-start.1 = ((bf16[4,4,72,256]{3,2,1,0:T(8,128)(2,1)}), bf16[4,4,72,256]{3,2,1,0:T(8,128)(2,1)}, u32[]{:S(2)}, u32[]{:S(2)}) async-start(bf16[4,4,72,256]{3,2,1,0:T(8,128)(2,1)} %bitcast.127), calls=%async_computation.1 | async-start | bytes 1179648 | tf_op jit(solution)/shard_map/all_to_all | solution.py:76
  35.1 11.7 %all-to-all-start.2 = ((bf16[4,4,72,256]{3,2,1,0:T(8,128)(2,1)}), bf16[4,4,72,256]{3,2,1,0:T(8,128)(2,1)}, u32[]{:S(2)}, u32[]{:S(2)}) async-start(bf16[4,4,72,256]{3,2,1,0:T(8,128)(2,1)} %bitcast.126), calls=%async_computation.2 | async-start | bytes 1179648 | tf_op jit(solution)/shard_map/all_to_all | solution.py:77
  95.6 6.8 %copy-start.6 = (s32[8,1]{0,1:T(1,128)S(1)}, s32[8,1]{0,1:T(1,128)}, u32[]{:S(2)}) copy-start(s32[8,1]{0,1:T(1,128)} %param.30) | copy-start | bytes 100
  97.9 17.4 %copy-start.7 = (f32[1152]{0:T(1024)S(1)}, f32[1152]{0:T(1024)}, u32[]{:S(2)}) copy-start(f32[1152]{0:T(1024)} %param.24) | copy-start | bytes 13828
  97.9 15.9 %all-to-all-start.3 = ((bf16[1,4,72,1024]{2,1,0,3:T(4,128)(2,1)}), bf16[1,4,72,1024]{2,1,0,3:T(4,128)(2,1)}, u32[]{:S(2)}, u32[]{:S(2)}) async-start(bf16[1,4,72,1024]{2,1,0,3:T(4,128)(2,1)} %bitcast.123), calls=%async_computation.3 | async-start | bytes 2097152 | tf_op jit(solution)/shard_map/all_to_all | solution.py:80
  102.3 144.5 %all-gather.3.cloned.1.call-start = ((), (), s32[]{:S(2)}) async-start(), calls=%async_computation.7 | async-start | bytes 8847360 | tf_op jit(solution)/shard_map/all_gather | solution.py:100
  118.4 1.1 copy-start.1
  172.1 0.7 copy-start.4
  172.1 134.3 %reduce-scatter.4.cloned.1.call-start = ((), (), s32[]{:S(2)}) async-start(), calls=%async_computation.9 | async-start | bytes 2211840
  273.8 113.4 %all-gather.5.cloned.1.call-start = ((), (), s32[]{:S(2)}) async-start(), calls=%async_computation.8 | async-start | bytes 2949120 | tf_op jit(solution)/shard_map/all_gather | solution.py:119
  344.7 7.4 %copy-start.2 = (bf16[1152,8]{0,1:T(8,128)(2,1)S(1)}, bf16[1152,8]{0,1:T(8,128)(2,1)}, u32[]{:S(2)}) copy-start(bf16[1152,8]{0,1:T(8,128)(2,1)} %param.25) | copy-start | bytes 55300
Sparse Core Ops, SparseCore 0:
  172.3 74.5 all-gather.2
  274.0 32.4 reduce-scatter.3
  351.9 35.2 all-gather.4
